TPU v7x, 128 devices: a whole 4x4x4 slice. The times are simulated.
128 devices in a mesh: segment: 4 (over x_lo, core), patch: 32 (over x_hi, y, z).
Axes of the slice: x: 4 (x_hi: 2, x_lo: 2; x = x_hi * 2 + x_lo), y: 4, z: 4, core: 2. Of those that a mesh axis runs over, the one named last changes fastest.
Arguments:
- features: bfloat16 [128, 28, 4, 12, 128], P('patch'), may hold values from -6 to 6
- deep_path: bfloat16 [128, 28, 4, 12, 128], P('patch'), may hold values from -6 to 6
- weight_first: bfloat16 [9, 28, 28], replicated, may hold values from -0.375 to 0.375
- bias_first: float32 [28], replicated, may hold values from -3 to 3
- weight_second: bfloat16 [27, 28, 28], replicated, may hold values from -0.21875 to 0.21875
- bias_second: float32 [28], replicated, may hold values from -3 to 3
- weight_third: bfloat16 [27, 28, 56], replicated, may hold values from -0.15625 to 0.15625
- bias_third: float32 [28], replicated, may hold values from -3 to 3
- weight_fourth: bfloat16 [27, 28, 56], replicated, may hold values from -0.15625 to 0.15625
- bias_fourth: float32 [28], replicated, may hold values from -3 to 3
- head_weight: bfloat16 [3, 28], replicated, may hold values from -2 to 2
- head_bias: float32 [3], replicated, may hold values from -3 to 3
- block_first: int32 [128], replicated, may hold values from 0 to 252, as said below
- block_offset: int32 [128], replicated, may hold values from 0 to 3
Outputs:
- blended: float32 [8, 32, 3, 4, 4, 128], P(None, 'patch', None, 'segment')
Inputs may be any that keep to these rules, and one draw needn't show every extreme that they name: A patch touches only blocks block_first to block_first + 3, all inside the slab.
All inputs are finite; a program needn't handle non-finite values.
Results may differ from a plain program's by a relative error of at most 0.0022.
Values may be sent and summed in bfloat16 or wider, within the bound.
A program may use at most 64 MiB of HBM per device.

v0:
```python
import functools
import math

import jax
import jax.numpy as jnp
from jax import lax
from jax.experimental import pallas as pl
from jax.experimental.pallas import tpu as pltpu
from jax.sharding import PartitionSpec as P

bf16 = jnp.bfloat16
f32 = jnp.float32
ROWS = 24


def bump(n, length):
    return math.sin(math.pi * (n + 0.5) / length) ** 2


def conv_kernel(index, feat_hbm, deep_hbm, wf_hbm, ws_hbm, wt_hbm, wo_hbm,
                bf_ref, bs_ref, bt_ref, bo_ref, hw_ref, hb_ref, out_ref,
                fbuf, dbuf, wfb, wsb, wtb, wob, plane, b_feat, b_mid, b_top,
                z_first, z_second, z_third, z_fourth, z_head, sems):
    s = index()
    copies = [
        pltpu.make_async_copy(feat_hbm.at[s], fbuf, sems.at[0]),
        pltpu.make_async_copy(wf_hbm, wfb, sems.at[1]),
        pltpu.make_async_copy(ws_hbm, wsb, sems.at[2]),
        pltpu.make_async_copy(deep_hbm.at[s], dbuf, sems.at[3]),
        pltpu.make_async_copy(wt_hbm, wtb, sems.at[4]),
        pltpu.make_async_copy(wo_hbm, wob, sems.at[5]),
    ]
    for copy in copies:
        copy.start()

    for buf, parts in ((b_feat, 1), (b_mid, 2), (b_top, 2)):
        for side in (0, 13 * 128):
            buf[:, side:side + 128] = jnp.zeros((parts * 384, 128), bf16)
    for z in range(4):
        plane[z * 512 + 448:z * 512 + 512, :] = jnp.zeros((64, 128), f32)
    lane = lax.broadcasted_iota(jnp.int32, (128, 128), 1)
    row = lax.broadcasted_iota(jnp.int32, (128, 128), 0)

    def put(buf, row0, col0, v):
        left = jnp.where(lane > 0, pltpu.roll(v, 1, 1), 0.0)
        right = jnp.where(lane < 127, pltpu.roll(v, 127, 1), 0.0)
        buf[row0:row0 + 128, col0:col0 + 128] = left.astype(bf16)
        buf[row0 + 128:row0 + 256, col0:col0 + 128] = v.astype(bf16)
        buf[row0 + 256:row0 + 384, col0:col0 + 128] = right.astype(bf16)

    def relayout(src, buf, row0):
        for c in range(28):
            for z in range(4):
                base = (z * 32 + c) * 16
                plane[base:base + 12, :] = src[c, z].astype(f32)
        for a in range(12):
            put(buf, row0, (a + 1) * 128, plane[pl.ds(a, 128, stride=16), :])

    def expand(w, dst, parts, full):
        dst[...] = jnp.zeros(dst.shape, bf16)
        for t in range(9):
            da, dy = t // 3, t % 3
            for part in range(parts):
                base = ((da * parts + part) * 3 + dy) * 128
                for zo in range(4):
                    for zi in range(4):
                        if full and abs(zi - zo) > 1 or not full and zi != zo:
                            continue
                        tap = 9 * (zi - zo + 1) + t if full else t
                        dst[zo * 32:zo * 32 + 28, base + zi * 32:base + zi * 32 + 28] = (
                            w[tap, :, part * 28:part * 28 + 28])

    def column(ref):
        lanes = lax.broadcasted_iota(jnp.int32, (128, 28), 1)
        rows = lax.rem(lax.broadcasted_iota(jnp.int32, (128, 28), 0), 32)
        return jnp.sum(jnp.where(lanes == rows, ref[...], 0.0), axis=1, keepdims=True)

    def layer(src, row0, parts, weights, bias_ref, emit):
        k = parts * 384
        bias = column(bias_ref)
        for n in range(6):
            acc = None
            for da in range(3):
                part = jnp.dot(weights[:, da * k:(da + 1) * k],
                               src[row0:row0 + k, (2 * n + da) * 128:(2 * n + da + 2) * 128],
                               preferred_element_type=f32)
                acc = part if acc is None else acc + part
            acc = jnp.maximum(acc + bias, 0.0)
            emit(2 * n, acc[:, :128])
            emit(2 * n + 1, acc[:, 128:])

    copies[1].wait()
    expand(wfb, z_first, 1, False)
    copies[0].wait()
    relayout(fbuf, b_feat, 0)
    layer(b_feat, 0, 1, z_first, bf_ref,
          lambda a, v: put(b_top, 384, (a + 1) * 128, v))
    copies[2].wait()
    expand(wsb, z_second, 1, True)
    layer(b_top, 384, 1, z_second, bs_ref,
          lambda a, v: put(b_mid, 0, (a + 1) * 128, v))
    copies[3].wait()
    relayout(dbuf, b_mid, 384)
    copies[4].wait()
    expand(wtb, z_third, 2, True)
    layer(b_mid, 0, 2, z_third, bt_ref,
          lambda a, v: put(b_top, 0, (a + 1) * 128, v))
    copies[5].wait()
    expand(wob, z_fourth, 2, True)

    z_head[...] = jnp.zeros((16, 128), f32)
    head = hw_ref[...].astype(f32)
    for z in range(4):
        z_head[z * 3:z * 3 + 3, z * 32:z * 32 + 28] = head
    hweight = z_head[...].astype(bf16)
    hrow = lax.broadcasted_iota(jnp.int32, (16, 128), 0)
    hlane = lax.broadcasted_iota(jnp.int32, (16, 128), 1)
    kind = lax.rem(hrow, 3)
    hbias = jnp.where(kind == 0, hb_ref[0], jnp.where(kind == 1, hb_ref[1], hb_ref[2]))
    section = hrow // 3
    depth = jnp.where((section == 0) | (section == 3), bump(0, 4), bump(1, 4))
    wave = jnp.sin((hlane.astype(f32) + 0.5) * (math.pi / 128))
    window = depth * (wave * wave)
    out_ref[...] = jnp.zeros(out_ref.shape, f32)

    def finish(a, v):
        logits = jnp.dot(hweight, v.astype(bf16), preferred_element_type=f32) + hbias
        value = jax.nn.sigmoid(logits) * (window * bump(a, 12))
        out_ref[pl.ds(3 + a, 12, stride=ROWS), :] = value[:12]

    layer(b_top, 0, 2, z_fourth, bo_ref, finish)


def conv_call(index, features, deep, wf, bfi, ws, bs, wt, bt, wo, bo, hw, hb):
    hbm = pl.BlockSpec(memory_space=pl.ANY)
    vmem = pl.BlockSpec(memory_space=pltpu.VMEM)
    smem = pl.BlockSpec(memory_space=pltpu.SMEM)
    V = pltpu.VMEM
    return pl.pallas_call(
        functools.partial(conv_kernel, index),
        out_shape=jax.ShapeDtypeStruct((12 * ROWS, 128), f32),
        in_specs=[hbm] * 6 + [vmem] * 5 + [smem],
        out_specs=vmem,
        scratch_shapes=[
            V((28, 4, 12, 128), bf16), V((28, 4, 12, 128), bf16),
            V((9, 28, 28), bf16), V((27, 28, 28), bf16), V((27, 28, 56), bf16), V((27, 28, 56), bf16),
            V((2048, 128), f32),
            V((384, 1792), bf16), V((768, 1792), bf16), V((768, 1792), bf16),
            V((128, 1152), bf16), V((128, 1152), bf16), V((128, 2304), bf16), V((128, 2304), bf16),
            V((16, 128), f32),
            pltpu.SemaphoreType.DMA((6,)),
        ],
        compiler_params=pltpu.CompilerParams(vmem_limit_bytes=48 << 20),
    )(features, deep, wf, ws, wt, wo, bfi.reshape(1, 28), bs.reshape(1, 28), bt.reshape(1, 28),
      bo.reshape(1, 28), hw, hb)


MESH = pl.DeviceIdType.MESH


def exchange_kernel(first_ref, offset_ref, planes, out_ref,
                    send_a, recv_a, send_b, recv_b, sa_sem, ra_sem, sb_sem, rb_sem):
    seg = lax.axis_index("segment")
    patch = lax.axis_index("patch")
    group = patch // 4
    turn = patch % 4
    mine = turn * 4 + seg

    def near(j):
        return {"segment": j % 4, "patch": group * 4 + j // 4}

    def far(g):
        return {"segment": seg, "patch": g * 4 + turn}

    barrier = pltpu.get_barrier_semaphore()
    for d in range(1, 16):
        pl.semaphore_signal(barrier, inc=1, device_id=near((mine + d) % 16), device_id_type=MESH)
    for d in range(1, 8):
        pl.semaphore_signal(barrier, inc=1, device_id=far((group + d) % 8), device_id_type=MESH)

    own = patch * 4 + seg
    first = first_ref[own]
    shift = 3 - offset_ref[own]

    def piece(j):
        block = (j // 4 - first + 256) % 4
        start = shift + 4 * block
        return [planes[pl.ds((j % 4 * 3 + kind) * ROWS + start, 4), :] for kind in range(3)]

    pl.semaphore_wait(barrier, 22)
    stage_a = []
    for d in range(1, 16):
        j = (mine + d) % 16
        for kind, value in enumerate(piece(j)):
            send_a[16 * d + 4 * kind:16 * d + 4 * kind + 4, :] = value
        copy = pltpu.make_async_remote_copy(
            src_ref=send_a.at[pl.ds(16 * d, 16)],
            dst_ref=recv_a.at[pl.ds(pl.multiple_of(16 * mine, 16), 16)],
            send_sem=sa_sem.at[d], recv_sem=ra_sem.at[mine],
            device_id=near(j), device_id_type=MESH)
        copy.start()
        stage_a.append(copy)
    for kind, value in enumerate(piece(mine)):
        recv_a[pl.ds(16 * mine + 4 * kind, 4), :] = value

    spot = lax.broadcasted_iota(jnp.int32, (64, 16), 1)
    rank = lax.broadcasted_iota(jnp.int32, (64, 16), 0)
    slot = jnp.zeros((64, 16), jnp.int32)
    for j in range(16):
        begin = first_ref[group * 16 + j]
        block = begin + (turn - begin + 256) % 4
        slot = jnp.where(spot == j, block // 4, slot)
    hot = (slot == (rank % 8) * 8 + rank // 8).astype(f32).astype(bf16)
    hot = jnp.concatenate([hot, hot, hot], axis=1)

    for d in range(1, 16):
        j = (mine + 16 - d) % 16
        pltpu.make_async_remote_copy(
            src_ref=send_a.at[pl.ds(16 * d, 16)],
            dst_ref=recv_a.at[pl.ds(pl.multiple_of(16 * j, 16), 16)],
            send_sem=sa_sem.at[d], recv_sem=ra_sem.at[j],
            device_id=near(j), device_id_type=MESH).wait_recv()

    columns = []
    for r in range(12):
        x = recv_a[pl.ds(r, 16, stride=16), :]
        high = x.astype(bf16)
        rest = x - high.astype(f32)
        mid = rest.astype(bf16)
        low = (rest - mid.astype(f32)).astype(bf16)
        columns.append(jnp.dot(hot, jnp.concatenate([high, mid, low], axis=0), preferred_element_type=f32))
    for r in range(12):
        v = columns[r]
        v = (v * v).reshape(8, 8, 128).astype(bf16)
        send_b[:, :, r * 128:(r + 1) * 128] = v

    stage_b = []
    for d in range(1, 8):
        g = (group + d) % 8
        copy = pltpu.make_async_remote_copy(
            src_ref=send_b.at[g], dst_ref=recv_b.at[d],
            send_sem=sb_sem.at[d], recv_sem=rb_sem.at[d],
            device_id=far(g), device_id_type=MESH)
        copy.start()
        stage_b.append(copy)
    total = jnp.sqrt(send_b[group].astype(f32))
    for copy in stage_b:
        copy.wait_recv()
    for d in range(1, 8):
        total = total + jnp.sqrt(recv_b[d].astype(f32))
    for r in range(12):
        out_ref[:, r, :] = total[:, r * 128:(r + 1) * 128]
    for copy in stage_a + stage_b:
        copy.wait_send()


def exchange_call(planes, first, offset):
    vmem = pl.BlockSpec(memory_space=pltpu.VMEM)
    smem = pl.BlockSpec(memory_space=pltpu.SMEM)
    V = pltpu.VMEM
    dma = pltpu.SemaphoreType.DMA
    return pl.pallas_call(
        exchange_kernel,
        out_shape=jax.ShapeDtypeStruct((8, 12, 128), f32),
        in_specs=[smem, smem, vmem],
        out_specs=vmem,
        scratch_shapes=[
            V((256, 128), f32), V((256, 128), f32),
            V((8, 8, 1536), bf16), V((8, 8, 1536), bf16),
            dma((16,)), dma((16,)), dma((8,)), dma((8,)),
        ],
        compiler_params=pltpu.CompilerParams(collective_id=0, has_side_effects=True),
    )(first, offset, planes)


def per_device(features, deep_path, weight_first, bias_first, weight_second, bias_second,
               weight_third, bias_third, weight_fourth, bias_fourth, head_weight, head_bias,
               block_first, block_offset):
    planes = conv_call(lambda: lax.axis_index("segment"), features, deep_path,
                       weight_first, bias_first, weight_second, bias_second,
                       weight_third, bias_third, weight_fourth, bias_fourth, head_weight, head_bias)
    blended = exchange_call(planes, block_first, block_offset)
    return blended.reshape(8, 1, 3, 1, 4, 128)


def solution(mesh):
    placed = (P("patch"), P("patch")) + (P(),) * 12
    return jax.shard_map(
        per_device,
        mesh=mesh,
        in_specs=placed,
        out_specs=P(None, "patch", None, "segment", None, None),
        check_vma=False,
    )
```

profile of v0, /device:TPU:0, one launch (start us, length us, event | category | flops | bytes accessed | tf_op | source)
XLA Modules:
  0.0 34.9 jit_solution(3350225010010445035)
XLA Ops:
  0.0 0.0 copy-start.11
  0.0 2.0 %copy.18.feat_hbm = bf16[4,28,4,12,128]{4,3,2,1,0:T(8,128)(2,1)S(1)} copy(bf16[4,28,4,12,128]{4,2,3,1,0:T(4,128)(2,1)} %param.14) | data formatting | bytes 2752512 | tf_op args[0]
  2.0 0.0 copy-done.11
  2.0 0.0 copy-start.1
  2.0 0.0 copy-start.2
  2.0 0.0 copy-start.3
  2.0 0.0 copy-start.4
  2.0 0.0 copy-start.5
  2.0 0.0 copy-start.6
  2.1 0.0 copy-start.7
  2.1 0.0 copy-start.8
  2.1 0.0 copy-start.9
  2.1 0.0 copy-start.10
  2.1 0.5 %copy.19.deep_hbm = bf16[4,28,4,12,128]{4,3,2,1,0:T(8,128)(2,1)S(1)} copy(bf16[4,28,4,12,128]{4,2,3,1,0:T(4,128)(2,1)S(1)} %copy-done.11) | data formatting | bytes 2752512 | tf_op args[1]
  2.6 0.3 copy-done.1
  2.9 0.1 copy-done.2
  3.0 0.1 copy-done.3
  3.1 0.1 copy-done.4
  3.2 0.0 copy-done.5
  3.2 0.0 copy-done.6
  3.2 0.0 copy-done.7
  3.2 0.0 copy-done.8
  3.2 0.0 copy-done.9
  3.2 0.0 copy-done.10
  3.2 10.5 %shard_map.136.planes = f32[288,128]{1,0:T(8,128)S(1)} custom-call(bf16[4,28,4,12,128]{4,3,2,1,0:T(8,128)(2,1)S(1)} %copy.18.feat_hbm, bf16[4,28,4,12,128]{4,3,2,1,0:T(8,128)(2,1)S(1)} %copy.19.deep_hbm, bf16[9,28,28]{2,1,0:T(8,128)(2,1)S(1)} %copy-done.4, bf16[27,28,28]{2,1,0:T(8,128)(2,1)S(1)} %copy-done.1, bf16[27,28,56]{2,1,0:T(8,128)(2,1)S(1)} %copy-done.2, ...), custom_call_target="tpu_custom_call" | custom-call | tf_op jit(solution)/shard_map/pallas_call | solution.py:139
  13.8 0.0 copy-start
  13.8 0.6 %copy-done = f32[288,128]{1,0:T(8,128)} copy-done((f32[288,128]{1,0:T(8,128)}, f32[288,128]{1,0:T(8,128)S(1)}, u32[]{:S(2)}) %copy-start) | copy-done | bytes 147480
  14.4 19.0 %shard_map.137 = f32[8,12,128]{2,1,0:T(8,128)} custom-call(s32[128]{0:T(128)} %first_ref.1, s32[128]{0:T(128)} %offset_ref.1, f32[288,128]{1,0:T(8,128)} %copy-done), custom_call_target="tpu_custom_call" | custom-call | tf_op jit(solution)/shard_map/pallas_call | solution.py:262
  33.4 0.9 %copy.20 = f32[8,12,128]{2,0,1:T(8,128)S(1)} copy(f32[8,12,128]{2,1,0:T(8,128)} %shard_map.137) | data formatting | bytes 98304 | tf_op jit(solution)/shard_map/pallas_call | solution.py:262
  34.3 0.6 %copy.21 = f32[8,1,3,1,4,128]{5,4,3,2,1,0:T(4,128)} copy(f32[8,1,3,1,4,128]{5,0,4,3,2,1:T(8,128)S(1)} %bitcast.9) | data formatting | bytes 98304 | tf_op jit(solution)/shard_map/reshape | solution.py:283
Async XLA Ops:
  0.0 2.0 %copy-start.11 = (bf16[4,28,4,12,128]{4,2,3,1,0:T(4,128)(2,1)S(1)}, bf16[4,28,4,12,128]{4,2,3,1,0:T(4,128)(2,1)}, u32[]{:S(2)}) copy-start(bf16[4,28,4,12,128]{4,2,3,1,0:T(4,128)(2,1)} %param.15) | copy-start | bytes 4128772
  2.0 0.9 %copy-start.1 = (bf16[27,28,28]{2,1,0:T(8,128)(2,1)S(1)}, bf16[27,28,28]{2,1,0:T(8,128)(2,1)}, u32[]{:S(2)}) copy-start(bf16[27,28,28]{2,1,0:T(8,128)(2,1)} %ws_hbm.1) | copy-start | bytes 127012
  2.0 1.0 %copy-start.2 = (bf16[27,28,56]{2,1,0:T(8,128)(2,1)S(1)}, bf16[27,28,56]{2,1,0:T(8,128)(2,1)}, u32[]{:S(2)}) copy-start(bf16[27,28,56]{2,1,0:T(8,128)(2,1)} %wt_hbm.1) | copy-start | bytes 254020
  2.0 1.1 %copy-start.3 = (bf16[27,28,56]{2,1,0:T(8,128)(2,1)S(1)}, bf16[27,28,56]{2,1,0:T(8,128)(2,1)}, u32[]{:S(2)}) copy-start(bf16[27,28,56]{2,1,0:T(8,128)(2,1)} %wo_hbm.1) | copy-start | bytes 254020
  2.0 1.2 %copy-start.4 = (bf16[9,28,28]{2,1,0:T(8,128)(2,1)S(1)}, bf16[9,28,28]{2,1,0:T(8,128)(2,1)}, u32[]{:S(2)}) copy-start(bf16[9,28,28]{2,1,0:T(8,128)(2,1)} %wf_hbm.1) | copy-start | bytes 42340
  2.0 1.2 %copy-start.5 = (bf16[3,28]{1,0:T(4,128)(2,1)S(1)}, bf16[3,28]{1,0:T(4,128)(2,1)}, u32[]{:S(2)}) copy-start(bf16[3,28]{1,0:T(4,128)(2,1)} %hw_ref.1) | copy-start | bytes 508
  2.0 1.2 %copy-start.6 = (f32[28]{0:T(128)S(1)}, f32[28]{0:T(128)}, u32[]{:S(2)}) copy-start(f32[28]{0:T(128)} %param.17) | copy-start | bytes 340
  2.1 1.2 %copy-start.7 = (f32[28]{0:T(128)S(1)}, f32[28]{0:T(128)}, u32[]{:S(2)}) copy-start(f32[28]{0:T(128)} %param.19) | copy-start | bytes 340
  2.1 1.1 %copy-start.8 = (f32[28]{0:T(128)S(1)}, f32[28]{0:T(128)}, u32[]{:S(2)}) copy-start(f32[28]{0:T(128)} %param.21) | copy-start | bytes 340
  2.1 1.1 %copy-start.9 = (f32[28]{0:T(128)S(1)}, f32[28]{0:T(128)}, u32[]{:S(2)}) copy-start(f32[28]{0:T(128)} %param.23) | copy-start | bytes 340
  2.1 1.1 %copy-start.10 = (f32[3]{0:T(128)S(1)}, f32[3]{0:T(128)}, u32[]{:S(2)}) copy-start(f32[3]{0:T(128)} %hb_ref.1) | copy-start | bytes 40
  13.8 0.7 %copy-start = (f32[288,128]{1,0:T(8,128)}, f32[288,128]{1,0:T(8,128)S(1)}, u32[]{:S(2)}) copy-start(f32[288,128]{1,0:T(8,128)S(1)} %shard_map.136.planes) | copy-start | bytes 442372
where the time goes:
time: 35.3 us; the launch traced here: 34.9 us
  Pallas kernels  29.5 us (84%)
  local copies, waits for them, and re-layouts  5.25 us (15%)
    pallas_call x1, Pallas kernels, exchange_call(): pl.pallas_call(exchange_kernel, out_shape=jax.ShapeDtypeStruct((8, 12, 12...  19 us
    pallas_call x1, Pallas kernels, conv_call(): pl.pallas_call(functools.partial(conv_kernel, index), out_shape=jax.Shape...  10.5 us
    unnamed x26, local copies, waits for them, and re-layouts  3.76 us
    pallas_call x1, local copies, waits for them, and re-layouts, exchange_call(): pl.pallas_call(exchange_kernel, out_shape=jax.ShapeDtypeStruct((8, 12, 12...  0.86 us

commit v1 on v0

v1 whole, which is shorter than its diff:
```python
import math

import jax
import jax.numpy as jnp
from jax import lax
from jax.experimental import pallas as pl
from jax.experimental.pallas import tpu as pltpu
from jax.sharding import PartitionSpec as P

bf16 = jnp.bfloat16
f32 = jnp.float32
MESH = pl.DeviceIdType.MESH
ROWS = 24


def bump(n, length):
    return math.sin(math.pi * (n + 0.5) / length) ** 2


def copies_in(s, hbm, buffers, sems):
    sources = [ref.at[s] if i < 2 else ref for i, ref in enumerate(hbm)]
    copies = [pltpu.make_async_copy(src, dst, sems.at[i])
              for i, (src, dst) in enumerate(zip(sources, buffers))]
    for i in (2, 0, 6, 3, 7, 1, 4, 8, 5, 9, 10):
        copies[i].start()
    return copies


def convolve(copies, buffers, hb_ref, planes, plane, b_feat, b_mid, b_top,
             z_first, z_second, z_third, z_fourth, z_head):
    fbuf, dbuf, wfb, wsb, wtb, wob, bf_ref, bs_ref, bt_ref, bo_ref, hw_ref = buffers

    for buf, parts in ((b_feat, 1), (b_mid, 2), (b_top, 2)):
        for side in (0, 13 * 128):
            buf[:, side:side + 128] = jnp.zeros((parts * 384, 128), bf16)
    plane[1344:1536, :] = jnp.zeros((192, 128), f32)
    planes[...] = jnp.zeros(planes.shape, f32)
    lane = lax.broadcasted_iota(jnp.int32, (128, 128), 1)

    def put(buf, row0, col0, v):
        left = jnp.where(lane > 0, pltpu.roll(v, 1, 1), 0.0)
        right = jnp.where(lane < 127, pltpu.roll(v, 127, 1), 0.0)
        buf[row0:row0 + 128, col0:col0 + 128] = left.astype(bf16)
        buf[row0 + 128:row0 + 256, col0:col0 + 128] = v.astype(bf16)
        buf[row0 + 256:row0 + 384, col0:col0 + 128] = right.astype(bf16)

    def relayout(src, buf, row0):
        plane[:1344, :] = src[...].astype(f32)
        for a in range(12):
            cell = [plane[pl.ds(4 * a + z, 32, stride=48), :] for z in range(4)]
            put(buf, row0, (a + 1) * 128, jnp.concatenate(cell, axis=0))

    def expand(w, dst, parts, full):
        dst[...] = jnp.zeros(dst.shape, bf16)
        for t in range(9):
            da, dy = t // 3, t % 3
            for part in range(parts):
                base = ((da * parts + part) * 3 + dy) * 128
                for zo in range(4):
                    for zi in range(4):
                        if abs(zi - zo) > (1 if full else 0):
                            continue
                        tap = 9 * (zi - zo + 1) + t if full else t
                        dst[zo * 32:zo * 32 + 28, base + zi * 32:base + zi * 32 + 28] = (
                            w[tap, :, part * 28:part * 28 + 28])

    def column(ref):
        lanes = lax.broadcasted_iota(jnp.int32, (128, 28), 1)
        rows = lax.rem(lax.broadcasted_iota(jnp.int32, (128, 28), 0), 32)
        return jnp.sum(jnp.where(lanes == rows, ref[...], 0.0), axis=1, keepdims=True)

    def layer(src, row0, parts, weights, bias_ref, emit):
        k = parts * 384
        bias = column(bias_ref)
        for n in range(6):
            acc = None
            for da in range(3):
                part = jnp.dot(weights[:, da * k:(da + 1) * k],
                               src[row0:row0 + k, (2 * n + da) * 128:(2 * n + da + 2) * 128],
                               preferred_element_type=f32)
                acc = part if acc is None else acc + part
            acc = jnp.maximum(acc + bias, 0.0)
            emit(2 * n, acc[:, :128])
            emit(2 * n + 1, acc[:, 128:])

    copies[2].wait()
    expand(wfb, z_first, 1, False)
    copies[0].wait()
    relayout(fbuf, b_feat, 0)
    copies[6].wait()
    layer(b_feat, 0, 1, z_first, bf_ref, lambda a, v: put(b_top, 384, (a + 1) * 128, v))
    copies[3].wait()
    expand(wsb, z_second, 1, True)
    copies[7].wait()
    layer(b_top, 384, 1, z_second, bs_ref, lambda a, v: put(b_mid, 0, (a + 1) * 128, v))
    copies[1].wait()
    relayout(dbuf, b_mid, 384)
    copies[4].wait()
    expand(wtb, z_third, 2, True)
    copies[8].wait()
    layer(b_mid, 0, 2, z_third, bt_ref, lambda a, v: put(b_top, 0, (a + 1) * 128, v))
    copies[5].wait()
    expand(wob, z_fourth, 2, True)
    copies[9].wait()
    copies[10].wait()

    z_head[...] = jnp.zeros((16, 128), f32)
    head = hw_ref[...].astype(f32)
    for z in range(4):
        z_head[z * 3:z * 3 + 3, z * 32:z * 32 + 28] = head
    hweight = z_head[...].astype(bf16)
    hrow = lax.broadcasted_iota(jnp.int32, (16, 128), 0)
    hlane = lax.broadcasted_iota(jnp.int32, (16, 128), 1)
    kind = lax.rem(hrow, 3)
    hbias = jnp.where(kind == 0, hb_ref[0], jnp.where(kind == 1, hb_ref[1], hb_ref[2]))
    depth = jnp.where((hrow < 3) | (hrow >= 9), bump(0, 4), bump(1, 4))
    wave = jnp.sin((hlane.astype(f32) + 0.5) * (math.pi / 128))
    window = depth * (wave * wave)

    def finish(a, v):
        logits = jnp.dot(hweight, v.astype(bf16), preferred_element_type=f32) + hbias
        value = jax.nn.sigmoid(logits) * (window * bump(a, 12))
        planes[pl.ds(3 + a, 12, stride=ROWS), :] = value[:12]

    layer(b_top, 0, 2, z_fourth, bo_ref, finish)


def kernel(feat, deep, wf, ws, wt, wo, bf_, bs, bt, bo, hw, hb_ref, first_ref, offset_ref, out_ref,
           fbuf, dbuf, wfb, wsb, wtb, wob, bfb, bsb, btb, bob, hwb,
           planes, plane, b_feat, b_mid, b_top, z_first, z_second, z_third, z_fourth, z_head,
           send_a, recv_a, send_b, recv_b, in_sem, sa_sem, ra_sem, sb_sem, rb_sem):
    seg = lax.axis_index("segment")
    patch = lax.axis_index("patch")
    group = patch // 4
    turn = patch % 4
    mine = turn * 4 + seg

    buffers = (fbuf, dbuf, wfb, wsb, wtb, wob, bfb, bsb, btb, bob, hwb)
    copies = copies_in(seg, (feat, deep, wf, ws, wt, wo, bf_, bs, bt, bo, hw), buffers, in_sem)

    def near(j):
        return {"segment": j % 4, "patch": group * 4 + j // 4}

    def far(g):
        return {"segment": seg, "patch": g * 4 + turn}

    barrier = pltpu.get_barrier_semaphore()
    for d in range(1, 16):
        pl.semaphore_signal(barrier, inc=1, device_id=near((mine + d) % 16), device_id_type=MESH)
    for d in range(1, 8):
        pl.semaphore_signal(barrier, inc=1, device_id=far((group + d) % 8), device_id_type=MESH)

    convolve(copies, buffers, hb_ref, planes, plane, b_feat, b_mid, b_top,
             z_first, z_second, z_third, z_fourth, z_head)

    own = patch * 4 + seg
    first = first_ref[own]
    shift = 3 - offset_ref[own]

    def piece(j):
        start = shift + 4 * ((j // 4 - first + 256) % 4)
        return [planes[pl.ds((j % 4 * 3 + kind) * ROWS + start, 4), :] for kind in range(3)]

    pl.semaphore_wait(barrier, 22)
    stage_a = []
    for d in range(1, 16):
        j = (mine + d) % 16
        for kind, value in enumerate(piece(j)):
            send_a[16 * d + 4 * kind:16 * d + 4 * kind + 4, :] = value
        copy = pltpu.make_async_remote_copy(
            src_ref=send_a.at[pl.ds(16 * d, 16)],
            dst_ref=recv_a.at[pl.ds(pl.multiple_of(16 * mine, 16), 16)],
            send_sem=sa_sem.at[d], recv_sem=ra_sem.at[mine],
            device_id=near(j), device_id_type=MESH)
        copy.start()
        stage_a.append(copy)
    for kind, value in enumerate(piece(mine)):
        recv_a[pl.ds(16 * mine + 4 * kind, 4), :] = value

    spot = lax.broadcasted_iota(jnp.int32, (64, 16), 1)
    rank = lax.broadcasted_iota(jnp.int32, (64, 16), 0)
    slot = jnp.zeros((64, 16), jnp.int32)
    for j in range(16):
        begin = first_ref[group * 16 + j]
        block = begin + (turn - begin + 256) % 4
        slot = jnp.where(spot == j, block // 4, slot)
    hot = (slot == (rank % 8) * 8 + rank // 8).astype(f32).astype(bf16)
    hot = jnp.concatenate([hot, hot, hot], axis=1)

    for d in range(1, 16):
        j = (mine + 16 - d) % 16
        pltpu.make_async_remote_copy(
            src_ref=send_a.at[pl.ds(16 * d, 16)],
            dst_ref=recv_a.at[pl.ds(pl.multiple_of(16 * j, 16), 16)],
            send_sem=sa_sem.at[d], recv_sem=ra_sem.at[j],
            device_id=near(j), device_id_type=MESH).wait_recv()

    sums = []
    for r in range(12):
        x = recv_a[pl.ds(r, 16, stride=16), :]
        high = x.astype(bf16)
        rest = x - high.astype(f32)
        mid = rest.astype(bf16)
        low = (rest - mid.astype(f32)).astype(bf16)
        sums.append(jnp.dot(hot, jnp.concatenate([high, mid, low], axis=0), preferred_element_type=f32))
    for r in range(12):
        send_b[:, :, r * 128:(r + 1) * 128] = (sums[r] * sums[r]).reshape(8, 8, 128).astype(bf16)

    stage_b = []
    for d in range(1, 8):
        g = (group + d) % 8
        copy = pltpu.make_async_remote_copy(
            src_ref=send_b.at[g], dst_ref=recv_b.at[d],
            send_sem=sb_sem.at[d], recv_sem=rb_sem.at[d],
            device_id=far(g), device_id_type=MESH)
        copy.start()
        stage_b.append(copy)
    total = jnp.sqrt(send_b[group].astype(f32))
    for copy in stage_b:
        copy.wait_recv()
    for d in range(1, 8):
        total = total + jnp.sqrt(recv_b[d].astype(f32))
    for r in range(12):
        out_ref[pl.ds(r, 8, stride=12), :] = total[:, r * 128:(r + 1) * 128]
    for copy in stage_a + stage_b:
        copy.wait_send()


def per_device(features, deep_path, weight_first, bias_first, weight_second, bias_second,
               weight_third, bias_third, weight_fourth, bias_fourth, head_weight, head_bias,
               block_first, block_offset):
    def rows(x):
        return x.transpose(0, 1, 3, 2, 4).reshape(4, 1344, 128)

    hbm = pl.BlockSpec(memory_space=pltpu.HBM)
    vmem = pl.BlockSpec(memory_space=pltpu.VMEM)
    smem = pl.BlockSpec(memory_space=pltpu.SMEM)
    V = pltpu.VMEM
    dma = pltpu.SemaphoreType.DMA
    blended = pl.pallas_call(
        kernel,
        out_shape=jax.ShapeDtypeStruct((96, 128), f32),
        in_specs=[hbm] * 11 + [smem] * 3,
        out_specs=vmem,
        scratch_shapes=[
            V((1344, 128), bf16), V((1344, 128), bf16),
            V((9, 28, 28), bf16), V((27, 28, 28), bf16), V((27, 28, 56), bf16), V((27, 28, 56), bf16),
            V((1, 28), f32), V((1, 28), f32), V((1, 28), f32), V((1, 28), f32), V((3, 28), bf16),
            V((12 * ROWS, 128), f32), V((1536, 128), f32),
            V((384, 1792), bf16), V((768, 1792), bf16), V((768, 1792), bf16),
            V((128, 1152), bf16), V((128, 1152), bf16), V((128, 2304), bf16), V((128, 2304), bf16),
            V((16, 128), f32),
            V((256, 128), f32), V((256, 128), f32), V((8, 8, 1536), bf16), V((8, 8, 1536), bf16),
            dma((11,)), dma((16,)), dma((16,)), dma((8,)), dma((8,)),
        ],
        compiler_params=pltpu.CompilerParams(
            collective_id=0, has_side_effects=True, vmem_limit_bytes=60 << 20),
    )(rows(features), rows(deep_path), weight_first, weight_second, weight_third, weight_fourth,
      bias_first.reshape(1, 28), bias_second.reshape(1, 28), bias_third.reshape(1, 28),
      bias_fourth.reshape(1, 28), head_weight, head_bias, block_first, block_offset)
    return blended.reshape(8, 1, 3, 1, 4, 128)


def solution(mesh):
    placed = (P("patch"), P("patch")) + (P(),) * 12
    return jax.shard_map(
        per_device,
        mesh=mesh,
        in_specs=placed,
        out_specs=P(None, "patch", None, "segment", None, None),
        check_vma=False,
    )
```

time: 35.3 us -> 27.7 us (0.78)
  local copies, waits for them, and re-layouts: 5.25 us -> 1.42 us
  Pallas kernels: 29.5 us -> 26.1 us
    pallas_call x2 -> x1, Pallas kernels: 29.5 us -> 26.1 us  [per_device(): pl.pallas_call(kernel, out_shape=jax.ShapeDtypeStruct((96, 128), f32), in...]
    unnamed x26 -> x1, local copies, waits for them, and re-layouts: 3.76 us -> 1.42 us
    pallas_call x1 -> x0, local copies, waits for them, and re-layouts: 0.86 us -> none  [exchange_call(): pl.pallas_call(exchange_kernel, out_shape=jax.ShapeDtypeStruct((8, 12, 12...]
    reshape x1 -> x0, local copies, waits for them, and re-layouts: 0.63 us -> none  [per_device(): return blended.reshape(8, 1, 3, 1, 4, 128)]
where the time goes in v1:
time: 27.7 us; the launch traced here: 27.6 us
  Pallas kernels  26.1 us (94%)
  local copies, waits for them, and re-layouts  1.42 us (5%)
    pallas_call x1, Pallas kernels, per_device(): pl.pallas_call(kernel, out_shape=jax.ShapeDtypeStruct((96, 128), f32), in...  26.1 us
    unnamed x1, local copies, waits for them, and re-layouts  1.42 us

profile of v1, /device:TPU:0, one launch (start us, length us, event | category | flops | bytes accessed | tf_op | source)
XLA Modules:
  0.0 27.6 jit_solution(178470514619574944)
XLA Ops:
  0.0 26.1 %shard_map.136 = f32[96,128]{1,0:T(8,128)} custom-call(bf16[4,1344,128]{2,1,0:T(8,128)(2,1)} %bitcast.13, bf16[4,1344,128]{2,1,0:T(8,128)(2,1)} %bitcast.14, bf16[9,28,28]{2,1,0:T(8,128)(2,1)} %wf.1, bf16[27,28,28]{2,1,0:T(8,128)(2,1)} %ws.1, bf16[27,28,56]{2,1,0:T(8,128)(2,1)} %wt.1, bf16[27,28,56]{2,1,0:T(8,128)(2,1)} %wo.1, f32[1,28]{1,0:T(1,128)} %bitcast.16, ...), custom_call_target="tpu_custom_call" | custom-call | tf_op jit(solution)/shard_map/pallas_call | solution.py:240
  26.1 1.4 %copy.17 = f32[8,1,3,1,4,128]{5,4,3,2,1,0:T(4,128)} copy(f32[8,1,3,1,4,128]{5,4,3,2,1,0:T(4,128)} %bitcast.15) | data formatting | bytes 98304

commit v2 on v1

--- a/solution.py
+++ b/solution.py
@@ -30,77 +30,89 @@
              z_first, z_second, z_third, z_fourth, z_head):
     fbuf, dbuf, wfb, wsb, wtb, wob, bf_ref, bs_ref, bt_ref, bo_ref, hw_ref = buffers
 
-    for buf, parts in ((b_feat, 1), (b_mid, 2), (b_top, 2)):
-        for side in (0, 13 * 128):
-            buf[:, side:side + 128] = jnp.zeros((parts * 384, 128), bf16)
     plane[1344:1536, :] = jnp.zeros((192, 128), f32)
     planes[...] = jnp.zeros(planes.shape, f32)
     lane = lax.broadcasted_iota(jnp.int32, (128, 128), 1)
 
     def put(buf, row0, col0, v):
-        left = jnp.where(lane > 0, pltpu.roll(v, 1, 1), 0.0)
-        right = jnp.where(lane < 127, pltpu.roll(v, 127, 1), 0.0)
-        buf[row0:row0 + 128, col0:col0 + 128] = left.astype(bf16)
-        buf[row0 + 128:row0 + 256, col0:col0 + 128] = v.astype(bf16)
-        buf[row0 + 256:row0 + 384, col0:col0 + 128] = right.astype(bf16)
+        v = v.astype(bf16)
+        zero = jnp.zeros((128, 128), bf16)
+        buf[row0:row0 + 128, col0:col0 + 128] = jnp.where(lane > 0, pltpu.roll(v, 1, 1), zero)
+        buf[row0 + 128:row0 + 256, col0:col0 + 128] = v
+        buf[row0 + 256:row0 + 384, col0:col0 + 128] = jnp.where(lane < 127, pltpu.roll(v, 127, 1), zero)
 
     def relayout(src, buf, row0):
-        plane[:1344, :] = src[...].astype(f32)
+        for c in range(0, 1344, 336):
+            plane[c:c + 336, :] = src[c:c + 336, :].astype(f32)
+            yield
         for a in range(12):
             cell = [plane[pl.ds(4 * a + z, 32, stride=48), :] for z in range(4)]
-            put(buf, row0, (a + 1) * 128, jnp.concatenate(cell, axis=0))
+            put(buf, row0, a * 128, jnp.concatenate(cell, axis=0))
+            yield
 
     def expand(w, dst, parts, full):
         dst[...] = jnp.zeros(dst.shape, bf16)
         for t in range(9):
             da, dy = t // 3, t % 3
             for part in range(parts):
-                base = ((da * parts + part) * 3 + dy) * 128
+                base = (part * 3 + dy) * 128
                 for zo in range(4):
                     for zi in range(4):
                         if abs(zi - zo) > (1 if full else 0):
                             continue
                         tap = 9 * (zi - zo + 1) + t if full else t
-                        dst[zo * 32:zo * 32 + 28, base + zi * 32:base + zi * 32 + 28] = (
+                        dst[da * 128 + zo * 32:da * 128 + zo * 32 + 28, base + zi * 32:base + zi * 32 + 28] = (
                             w[tap, :, part * 28:part * 28 + 28])
+                yield
 
     def column(ref):
         lanes = lax.broadcasted_iota(jnp.int32, (128, 28), 1)
         rows = lax.rem(lax.broadcasted_iota(jnp.int32, (128, 28), 0), 32)
         return jnp.sum(jnp.where(lanes == rows, ref[...], 0.0), axis=1, keepdims=True)
 
-    def layer(src, row0, parts, weights, bias_ref, emit):
+    def layer(src, row0, parts, weights, bias_ref, emit, beside=()):
         k = parts * 384
         bias = column(bias_ref)
+        sums = {}
         for n in range(6):
-            acc = None
-            for da in range(3):
-                part = jnp.dot(weights[:, da * k:(da + 1) * k],
-                               src[row0:row0 + k, (2 * n + da) * 128:(2 * n + da + 2) * 128],
-                               preferred_element_type=f32)
-                acc = part if acc is None else acc + part
-            acc = jnp.maximum(acc + bias, 0.0)
-            emit(2 * n, acc[:, :128])
-            emit(2 * n + 1, acc[:, 128:])
+            p = jnp.dot(weights[...], src[row0:row0 + k, n * 256:(n + 1) * 256],
+                        preferred_element_type=f32)
+            for task, count in beside:
+                for _ in range(count):
+                    next(task, None)
+            for b in (2 * n, 2 * n + 1):
+                for da in (2, 1, 0):
+                    a = b + 1 - da
+                    if 0 <= a < 12:
+                        term = p[da * 128:(da + 1) * 128, (b - 2 * n) * 128:(b - 2 * n + 1) * 128]
+                        sums[a] = sums[a] + term if a in sums else term
+            for a in (2 * n - 1, 2 * n) + ((11,) if n == 5 else ()):
+                if a >= 0:
+                    emit(a, jnp.maximum(sums.pop(a) + bias, 0.0))
+
+    def run(task):
+        for _ in task:
+            pass
 
     copies[2].wait()
-    expand(wfb, z_first, 1, False)
+    run(expand(wfb, z_first, 1, False))
     copies[0].wait()
-    relayout(fbuf, b_feat, 0)
-    copies[6].wait()
-    layer(b_feat, 0, 1, z_first, bf_ref, lambda a, v: put(b_top, 384, (a + 1) * 128, v))
-    copies[3].wait()
-    expand(wsb, z_second, 1, True)
-    copies[7].wait()
-    layer(b_top, 384, 1, z_second, bs_ref, lambda a, v: put(b_mid, 0, (a + 1) * 128, v))
-    copies[1].wait()
-    relayout(dbuf, b_mid, 384)
-    copies[4].wait()
-    expand(wtb, z_third, 2, True)
-    copies[8].wait()
-    layer(b_mid, 0, 2, z_third, bt_ref, lambda a, v: put(b_top, 0, (a + 1) * 128, v))
-    copies[5].wait()
-    expand(wob, z_fourth, 2, True)
+    run(relayout(fbuf, b_feat, 0))
+    for i in (6, 3, 7, 1):
+        copies[i].wait()
+    second = expand(wsb, z_second, 1, True)
+    deeper = relayout(dbuf, b_mid, 384)
+    layer(b_feat, 0, 1, z_first, bf_ref, lambda a, v: put(b_top, 384, a * 128, v), [(second, 2), (deeper, 2)])
+    run(second)
+    for i in (4, 8, 5):
+        copies[i].wait()
+    third = expand(wtb, z_third, 2, True)
+    fourth = expand(wob, z_fourth, 2, True)
+    layer(b_top, 384, 1, z_second, bs_ref, lambda a, v: put(b_mid, 0, a * 128, v), [(deeper, 3), (third, 3)])
+    run(deeper)
+    run(third)
+    layer(b_mid, 0, 2, z_third, bt_ref, lambda a, v: put(b_top, 0, a * 128, v), [(fourth, 3)])
+    run(fourth)
     copies[9].wait()
     copies[10].wait()
 
@@ -117,12 +129,14 @@
     wave = jnp.sin((hlane.astype(f32) + 0.5) * (math.pi / 128))
     window = depth * (wave * wave)
 
-    def finish(a, v):
-        logits = jnp.dot(hweight, v.astype(bf16), preferred_element_type=f32) + hbias
-        value = jax.nn.sigmoid(logits) * (window * bump(a, 12))
+    def keep(a, v):
+        b_feat[0:128, a * 128:(a + 1) * 128] = v.astype(bf16)
+
+    layer(b_top, 0, 2, z_fourth, bo_ref, keep)
+    logits = jnp.dot(hweight, b_feat[0:128, :], preferred_element_type=f32)
+    for a in range(12):
+        value = jax.nn.sigmoid(logits[:, a * 128:(a + 1) * 128] + hbias) * (window * bump(a, 12))
         planes[pl.ds(3 + a, 12, stride=ROWS), :] = value[:12]
-
-    layer(b_top, 0, 2, z_fourth, bo_ref, finish)
 
 
 def kernel(feat, deep, wf, ws, wt, wo, bf_, bs, bt, bo, hw, hb_ref, first_ref, offset_ref, out_ref,
@@ -226,6 +240,25 @@
         copy.wait_send()
 
 
+def conv_buffers():
+    V = pltpu.VMEM
+    return [
+        V((1344, 128), bf16), V((1344, 128), bf16),
+        V((9, 28, 28), bf16), V((27, 28, 28), bf16), V((27, 28, 56), bf16), V((27, 28, 56), bf16),
+        V((1, 28), f32), V((1, 28), f32), V((1, 28), f32), V((1, 28), f32), V((3, 28), bf16),
+    ]
+
+
+def conv_scratch():
+    V = pltpu.VMEM
+    return [
+        V((1536, 128), f32),
+        V((384, 1536), bf16), V((768, 1536), bf16), V((768, 1536), bf16),
+        V((384, 384), bf16), V((384, 384), bf16), V((384, 768), bf16), V((384, 768), bf16),
+        V((16, 128), f32),
+    ]
+
+
 def per_device(features, deep_path, weight_first, bias_first, weight_second, bias_second,
                weight_third, bias_third, weight_fourth, bias_fourth, head_weight, head_bias,
                block_first, block_offset):
@@ -242,14 +275,7 @@
         out_shape=jax.ShapeDtypeStruct((96, 128), f32),
         in_specs=[hbm] * 11 + [smem] * 3,
         out_specs=vmem,
-        scratch_shapes=[
-            V((1344, 128), bf16), V((1344, 128), bf16),
-            V((9, 28, 28), bf16), V((27, 28, 28), bf16), V((27, 28, 56), bf16), V((27, 28, 56), bf16),
-            V((1, 28), f32), V((1, 28), f32), V((1, 28), f32), V((1, 28), f32), V((3, 28), bf16),
-            V((12 * ROWS, 128), f32), V((1536, 128), f32),
-            V((384, 1792), bf16), V((768, 1792), bf16), V((768, 1792), bf16),
-            V((128, 1152), bf16), V((128, 1152), bf16), V((128, 2304), bf16), V((128, 2304), bf16),
-            V((16, 128), f32),
+        scratch_shapes=conv_buffers() + [V((12 * ROWS, 128), f32)] + conv_scratch() + [
             V((256, 128), f32), V((256, 128), f32), V((8, 8, 1536), bf16), V((8, 8, 1536), bf16),
             dma((11,)), dma((16,)), dma((16,)), dma((8,)), dma((8,)),
         ],

time: 27.7 us -> 24 us (0.87)
  Pallas kernels: 26.1 us -> 22.4 us
    pallas_call x1, Pallas kernels: 26.1 us -> 22.4 us  [per_device(): pl.pallas_call(kernel, out_shape=jax.ShapeDtypeStruct((96, 128), f32), in...]
where the time goes in v2:
time: 24 us; the launch traced here: 23.8 us
  Pallas kernels  22.4 us (93%)
  local copies, waits for them, and re-layouts  1.42 us (6%)
    pallas_call x1, Pallas kernels, per_device(): pl.pallas_call(kernel, out_shape=jax.ShapeDtypeStruct((96, 128), f32), in...  22.4 us
    unnamed x1, local copies, waits for them, and re-layouts  1.42 us

profile of v2, /device:TPU:0, one launch (start us, length us, event | category | flops | bytes accessed | tf_op | source)
XLA Modules:
  0.0 23.8 jit_solution(13043168389014443231)
XLA Ops:
  0.0 22.4 %shard_map.136 = f32[96,128]{1,0:T(8,128)} custom-call(bf16[4,1344,128]{2,1,0:T(8,128)(2,1)} %bitcast.13, bf16[4,1344,128]{2,1,0:T(8,128)(2,1)} %bitcast.14, bf16[9,28,28]{2,1,0:T(8,128)(2,1)} %wf.1, bf16[27,28,28]{2,1,0:T(8,128)(2,1)} %ws.1, bf16[27,28,56]{2,1,0:T(8,128)(2,1)} %wt.1, bf16[27,28,56]{2,1,0:T(8,128)(2,1)} %wo.1, f32[1,28]{1,0:T(1,128)} %bitcast.16, ...), custom_call_target="tpu_custom_call" | custom-call | tf_op jit(solution)/shard_map/pallas_call | solution.py:273
  22.4 1.4 %copy.17 = f32[8,1,3,1,4,128]{5,4,3,2,1,0:T(4,128)} copy(f32[8,1,3,1,4,128]{5,4,3,2,1,0:T(4,128)} %bitcast.15) | data formatting | bytes 98304

commit v3 on v2

--- a/solution.py
+++ b/solution.py
@@ -142,27 +142,40 @@
 def kernel(feat, deep, wf, ws, wt, wo, bf_, bs, bt, bo, hw, hb_ref, first_ref, offset_ref, out_ref,
            fbuf, dbuf, wfb, wsb, wtb, wob, bfb, bsb, btb, bob, hwb,
            planes, plane, b_feat, b_mid, b_top, z_first, z_second, z_third, z_fourth, z_head,
-           send_a, recv_a, send_b, recv_b, in_sem, sa_sem, ra_sem, sb_sem, rb_sem):
+           hot_ref, send_a, recv_a, pieces, send_b, recv_b, in_sem, sa_sem, ra_sem, sb_sem, rb_sem):
     seg = lax.axis_index("segment")
     patch = lax.axis_index("patch")
-    group = patch // 4
+    half = patch // 16
+    line = patch // 4 % 4
     turn = patch % 4
     mine = turn * 4 + seg
 
     buffers = (fbuf, dbuf, wfb, wsb, wtb, wob, bfb, bsb, btb, bob, hwb)
     copies = copies_in(seg, (feat, deep, wf, ws, wt, wo, bf_, bs, bt, bo, hw), buffers, in_sem)
 
-    def near(j):
-        return {"segment": j % 4, "patch": group * 4 + j // 4}
-
-    def far(g):
-        return {"segment": seg, "patch": g * 4 + turn}
-
+    def near(h, j):
+        return {"segment": j % 4, "patch": (h * 4 + line) * 4 + j // 4}
+
+    def along(y):
+        return {"segment": seg, "patch": (half * 4 + y) * 4 + turn}
+
+    others = [(h, d) for h in (1, 0) for d in range(16) if h or d]
     barrier = pltpu.get_barrier_semaphore()
-    for d in range(1, 16):
-        pl.semaphore_signal(barrier, inc=1, device_id=near((mine + d) % 16), device_id_type=MESH)
-    for d in range(1, 8):
-        pl.semaphore_signal(barrier, inc=1, device_id=far((group + d) % 8), device_id_type=MESH)
+    for h, d in others:
+        pl.semaphore_signal(barrier, inc=1, device_id=near((half + h) % 2, (mine + d) % 16),
+                            device_id_type=MESH)
+    for d in range(1, 4):
+        pl.semaphore_signal(barrier, inc=1, device_id=along((line + d) % 4), device_id_type=MESH)
+
+    spot = lax.broadcasted_iota(jnp.int32, (32, 32), 1)
+    rank = lax.broadcasted_iota(jnp.int32, (32, 32), 0)
+    slot = jnp.zeros((32, 32), jnp.int32)
+    for j in range(32):
+        begin = first_ref[(j // 16 * 4 + line) * 16 + j % 16]
+        block = begin + (turn - begin + 256) % 4
+        slot = jnp.where(spot == j, block // 4, slot)
+    goal = (rank % 8) * 8 + half * 4 + (rank // 8 + line) % 4
+    hot_ref[...] = (slot == goal).astype(f32)
 
     convolve(copies, buffers, hb_ref, planes, plane, b_feat, b_mid, b_top,
              z_first, z_second, z_third, z_fourth, z_head)
@@ -173,67 +186,58 @@
 
     def piece(j):
         start = shift + 4 * ((j // 4 - first + 256) % 4)
-        return [planes[pl.ds((j % 4 * 3 + kind) * ROWS + start, 4), :] for kind in range(3)]
-
-    pl.semaphore_wait(barrier, 22)
+        value = jnp.concatenate(
+            [planes[pl.ds((j % 4 * 3 + kind) * ROWS + start, 4), :] for kind in range(3)], axis=0)
+        return (value * value).astype(bf16)
+
+    for d in range(16):
+        send_a[d] = piece((mine + d) % 16)
+    pl.semaphore_wait(barrier, 34)
     stage_a = []
-    for d in range(1, 16):
-        j = (mine + d) % 16
-        for kind, value in enumerate(piece(j)):
-            send_a[16 * d + 4 * kind:16 * d + 4 * kind + 4, :] = value
+    for n, (h, d) in enumerate(others):
         copy = pltpu.make_async_remote_copy(
-            src_ref=send_a.at[pl.ds(16 * d, 16)],
-            dst_ref=recv_a.at[pl.ds(pl.multiple_of(16 * mine, 16), 16)],
-            send_sem=sa_sem.at[d], recv_sem=ra_sem.at[mine],
-            device_id=near(j), device_id_type=MESH)
+            src_ref=send_a.at[d], dst_ref=recv_a.at[half * 16 + mine],
+            send_sem=sa_sem.at[n], recv_sem=ra_sem.at[half * 16 + mine],
+            device_id=near((half + h) % 2, (mine + d) % 16), device_id_type=MESH)
         copy.start()
         stage_a.append(copy)
-    for kind, value in enumerate(piece(mine)):
-        recv_a[pl.ds(16 * mine + 4 * kind, 4), :] = value
-
-    spot = lax.broadcasted_iota(jnp.int32, (64, 16), 1)
-    rank = lax.broadcasted_iota(jnp.int32, (64, 16), 0)
-    slot = jnp.zeros((64, 16), jnp.int32)
-    for j in range(16):
-        begin = first_ref[group * 16 + j]
-        block = begin + (turn - begin + 256) % 4
-        slot = jnp.where(spot == j, block // 4, slot)
-    hot = (slot == (rank % 8) * 8 + rank // 8).astype(f32).astype(bf16)
-    hot = jnp.concatenate([hot, hot, hot], axis=1)
-
-    for d in range(1, 16):
-        j = (mine + 16 - d) % 16
+    recv_a[half * 16 + mine] = send_a[0]
+    for n, (h, d) in enumerate(others):
+        j = (half + h) % 2 * 16 + (mine + 16 - d) % 16
         pltpu.make_async_remote_copy(
-            src_ref=send_a.at[pl.ds(16 * d, 16)],
-            dst_ref=recv_a.at[pl.ds(pl.multiple_of(16 * j, 16), 16)],
-            send_sem=sa_sem.at[d], recv_sem=ra_sem.at[j],
-            device_id=near(j), device_id_type=MESH).wait_recv()
-
-    sums = []
+            src_ref=send_a.at[d], dst_ref=recv_a.at[j],
+            send_sem=sa_sem.at[n], recv_sem=ra_sem.at[j],
+            device_id=near((half + h) % 2, (mine + 16 - d) % 16), device_id_type=MESH).wait_recv()
+
+    for j in range(32):
+        pieces[16 * j:16 * j + 12, :] = jnp.sqrt(recv_a[j].astype(f32))
+    hot = hot_ref[...].astype(bf16)
+    hot = jnp.concatenate([hot, hot], axis=1)
     for r in range(12):
-        x = recv_a[pl.ds(r, 16, stride=16), :]
+        x = pieces[pl.ds(r, 32, stride=16), :]
         high = x.astype(bf16)
-        rest = x - high.astype(f32)
-        mid = rest.astype(bf16)
-        low = (rest - mid.astype(f32)).astype(bf16)
-        sums.append(jnp.dot(hot, jnp.concatenate([high, mid, low], axis=0), preferred_element_type=f32))
-    for r in range(12):
-        send_b[:, :, r * 128:(r + 1) * 128] = (sums[r] * sums[r]).reshape(8, 8, 128).astype(bf16)
+        low = (x - high.astype(f32)).astype(bf16)
+        v = jnp.dot(hot, jnp.concatenate([high, low], axis=0), preferred_element_type=f32)
+        v = v * v
+        send_b[:, :, r * 128:(r + 1) * 128] = (v * v).reshape(4, 8, 128).astype(bf16)
 
     stage_b = []
-    for d in range(1, 8):
-        g = (group + d) % 8
+    for d in (2, 1, 3):
         copy = pltpu.make_async_remote_copy(
-            src_ref=send_b.at[g], dst_ref=recv_b.at[d],
+            src_ref=send_b.at[d], dst_ref=recv_b.at[d],
             send_sem=sb_sem.at[d], recv_sem=rb_sem.at[d],
-            device_id=far(g), device_id_type=MESH)
+            device_id=along((line + d) % 4), device_id_type=MESH)
         copy.start()
         stage_b.append(copy)
-    total = jnp.sqrt(send_b[group].astype(f32))
+
+    def decode(x):
+        return jnp.sqrt(jnp.sqrt(x.astype(f32)))
+
+    total = decode(send_b[0])
     for copy in stage_b:
         copy.wait_recv()
-    for d in range(1, 8):
-        total = total + jnp.sqrt(recv_b[d].astype(f32))
+    for d in range(1, 4):
+        total = total + decode(recv_b[d])
     for r in range(12):
         out_ref[pl.ds(r, 8, stride=12), :] = total[:, r * 128:(r + 1) * 128]
     for copy in stage_a + stage_b:
@@ -272,12 +276,13 @@
     dma = pltpu.SemaphoreType.DMA
     blended = pl.pallas_call(
         kernel,
-        out_shape=jax.ShapeDtypeStruct((96, 128), f32),
+        out_shape=V((96, 128), f32),
         in_specs=[hbm] * 11 + [smem] * 3,
         out_specs=vmem,
         scratch_shapes=conv_buffers() + [V((12 * ROWS, 128), f32)] + conv_scratch() + [
-            V((256, 128), f32), V((256, 128), f32), V((8, 8, 1536), bf16), V((8, 8, 1536), bf16),
-            dma((11,)), dma((16,)), dma((16,)), dma((8,)), dma((8,)),
+            V((32, 32), f32), V((16, 12, 128), bf16), V((32, 12, 128), bf16), V((512, 128), f32),
+            V((4, 8, 1536), bf16), V((4, 8, 1536), bf16),
+            dma((11,)), dma((31,)), dma((32,)), dma((4,)), dma((4,)),
         ],
         compiler_params=pltpu.CompilerParams(
             collective_id=0, has_side_effects=True, vmem_limit_bytes=60 << 20),

time: 24 us -> 22.2 us (0.925)
  Pallas kernels: 22.4 us -> 21.3 us
  local copies, waits for them, and re-layouts: 1.42 us -> 0.62 us
    pallas_call x1, Pallas kernels: 22.4 us -> 21.3 us  [per_device(): pl.pallas_call(kernel, out_shape=V((96, 128), f32), in_specs=[hbm] * 11 +...]
    unnamed x1, local copies, waits for them, and re-layouts: 1.42 us -> 0.62 us
where the time goes in v3:
time: 22.2 us; the launch traced here: 21.9 us
  Pallas kernels  21.3 us (96%)
  local copies, waits for them, and re-layouts  0.62 us (3%)
    pallas_call x1, Pallas kernels, per_device(): pl.pallas_call(kernel, out_shape=V((96, 128), f32), in_specs=[hbm] * 11 +...  21.3 us
    unnamed x1, local copies, waits for them, and re-layouts  0.62 us

profile of v3, /device:TPU:0, one launch (start us, length us, event | category | flops | bytes accessed | tf_op | source)
XLA Modules:
  0.0 21.9 jit_solution(4285584802325140025)
XLA Ops:
  0.0 21.3 %shard_map.136 = f32[96,128]{1,0:T(8,128)S(1)} custom-call(bf16[4,1344,128]{2,1,0:T(8,128)(2,1)} %bitcast.14, bf16[4,1344,128]{2,1,0:T(8,128)(2,1)} %bitcast.15, bf16[9,28,28]{2,1,0:T(8,128)(2,1)} %wf.1, bf16[27,28,28]{2,1,0:T(8,128)(2,1)} %ws.1, bf16[27,28,56]{2,1,0:T(8,128)(2,1)} %wt.1, bf16[27,28,56]{2,1,0:T(8,128)(2,1)} %wo.1, f32[1,28]{1,0:T(1,128)} %bitcast.16, ...), custom_call_target="tpu_custom_call" | custom-call | tf_op jit(solution)/shard_map/pallas_call | solution.py:277
  21.3 0.6 %copy.17 = f32[8,1,3,1,4,128]{5,4,3,2,1,0:T(4,128)} copy(f32[8,1,3,1,4,128]{5,4,3,2,1,0:T(4,128)S(1)} %bitcast.13) | data formatting | bytes 98304

commit v4 on v3

--- a/solution.py
+++ b/solution.py
@@ -9,7 +9,7 @@
 
 bf16 = jnp.bfloat16
 f32 = jnp.float32
-MESH = pl.DeviceIdType.MESH
+LOGICAL = pl.DeviceIdType.LOGICAL
 ROWS = 24
 
 
@@ -26,12 +26,14 @@
     return copies
 
 
-def convolve(copies, buffers, hb_ref, planes, plane, b_feat, b_mid, b_top,
+def convolve(copies, slots, buffers, hb_ref, planes, plane, b_feat, b_mid, b_top,
              z_first, z_second, z_third, z_fourth, z_head):
     fbuf, dbuf, wfb, wsb, wtb, wob, bf_ref, bs_ref, bt_ref, bo_ref, hw_ref = buffers
 
     plane[1344:1536, :] = jnp.zeros((192, 128), f32)
     planes[...] = jnp.zeros(planes.shape, f32)
+    for dst in (z_first, z_second, z_third, z_fourth):
+        dst[...] = jnp.zeros(dst.shape, bf16)
     lane = lax.broadcasted_iota(jnp.int32, (128, 128), 1)
 
     def put(buf, row0, col0, v):
@@ -51,7 +53,6 @@
             yield
 
     def expand(w, dst, parts, full):
-        dst[...] = jnp.zeros(dst.shape, bf16)
         for t in range(9):
             da, dy = t // 3, t % 3
             for part in range(parts):
@@ -104,6 +105,7 @@
     deeper = relayout(dbuf, b_mid, 384)
     layer(b_feat, 0, 1, z_first, bf_ref, lambda a, v: put(b_top, 384, a * 128, v), [(second, 2), (deeper, 2)])
     run(second)
+    slots()
     for i in (4, 8, 5):
         copies[i].wait()
     third = expand(wtb, z_third, 2, True)
@@ -139,75 +141,82 @@
         planes[pl.ds(3 + a, 12, stride=ROWS), :] = value[:12]
 
 
-def kernel(feat, deep, wf, ws, wt, wo, bf_, bs, bt, bo, hw, hb_ref, first_ref, offset_ref, out_ref,
-           fbuf, dbuf, wfb, wsb, wtb, wob, bfb, bsb, btb, bob, hwb,
+def kernel(feat, deep, wf, ws, wt, wo, bf_, bs, bt, bo, hw, hb, first_hbm, offset_hbm, out_ref,
+           fbuf, dbuf, wfb, wsb, wtb, wob, bfb, bsb, btb, bob, hwb, hb_ref, first_ref, offset_ref,
            planes, plane, b_feat, b_mid, b_top, z_first, z_second, z_third, z_fourth, z_head,
            hot_ref, send_a, recv_a, pieces, send_b, recv_b, in_sem, sa_sem, ra_sem, sb_sem, rb_sem):
     seg = lax.axis_index("segment")
     patch = lax.axis_index("patch")
-    half = patch // 16
-    line = patch // 4 % 4
-    turn = patch % 4
-    mine = turn * 4 + seg
+    half = lax.div(patch, 16)
+    line = lax.rem(lax.div(patch, 4), 4)
+    turn = lax.rem(patch, 4)
+    here = half * 16 + turn * 4 + seg
 
     buffers = (fbuf, dbuf, wfb, wsb, wtb, wob, bfb, bsb, btb, bob, hwb)
     copies = copies_in(seg, (feat, deep, wf, ws, wt, wo, bf_, bs, bt, bo, hw), buffers, in_sem)
-
-    def near(h, j):
-        return {"segment": j % 4, "patch": (h * 4 + line) * 4 + j // 4}
-
-    def along(y):
-        return {"segment": seg, "patch": (half * 4 + y) * 4 + turn}
-
-    others = [(h, d) for h in (1, 0) for d in range(16) if h or d]
+    tables = [pltpu.make_async_copy(src, dst, in_sem.at[11 + i]) for i, (src, dst) in enumerate(
+        ((hb, hb_ref), (first_hbm, first_ref), (offset_hbm, offset_ref)))]
+    for table in tables:
+        table.start()
+
+    halves = [half, 1 - half]
+    turns = [lax.rem(turn + d, 4) for d in range(4)]
+    segs = [lax.rem(seg + d, 4) for d in range(4)]
+    lines = [lax.rem(line + d, 4) for d in range(4)]
+
+    def device(h, y, t, s):
+        return s * 32 + h * 16 + y * 4 + t
+
+    others = [(h, t, s) for h in (1, 0) for t in (2, 1, 3, 0) for s in (2, 1, 3, 0) if h or t or s]
+    ids = [device(halves[h], line, turns[t], segs[s]) for h, t, s in others]
+    spots = [halves[h] * 16 + turns[t] * 4 + segs[s] for h, t, s in others]
     barrier = pltpu.get_barrier_semaphore()
-    for h, d in others:
-        pl.semaphore_signal(barrier, inc=1, device_id=near((half + h) % 2, (mine + d) % 16),
-                            device_id_type=MESH)
-    for d in range(1, 4):
-        pl.semaphore_signal(barrier, inc=1, device_id=along((line + d) % 4), device_id_type=MESH)
-
-    spot = lax.broadcasted_iota(jnp.int32, (32, 32), 1)
-    rank = lax.broadcasted_iota(jnp.int32, (32, 32), 0)
-    slot = jnp.zeros((32, 32), jnp.int32)
-    for j in range(32):
-        begin = first_ref[(j // 16 * 4 + line) * 16 + j % 16]
-        block = begin + (turn - begin + 256) % 4
-        slot = jnp.where(spot == j, block // 4, slot)
-    goal = (rank % 8) * 8 + half * 4 + (rank // 8 + line) % 4
-    hot_ref[...] = (slot == goal).astype(f32)
-
-    convolve(copies, buffers, hb_ref, planes, plane, b_feat, b_mid, b_top,
+    for peer in ids + [device(half, y, turn, seg) for y in lines[1:]]:
+        pl.semaphore_signal(barrier, inc=1, device_id=peer, device_id_type=LOGICAL)
+
+    def slots():
+        for table in tables:
+            table.wait()
+        spot = lax.broadcasted_iota(jnp.int32, (32, 32), 1)
+        rank = lax.broadcasted_iota(jnp.int32, (32, 32), 0)
+        slot = jnp.zeros((32, 32), jnp.int32)
+        for j in range(32):
+            begin = first_ref[(j // 16 * 4 + line) * 16 + j % 16]
+            block = begin + lax.rem(turn - begin + 256, 4)
+            slot = jnp.where(spot == j, lax.div(block, 4), slot)
+        goal = (rank % 8) * 8 + half * 4 + (rank // 8 + line) % 4
+        hot_ref[...] = (slot == goal).astype(f32)
+
+    convolve(copies, slots, buffers, hb_ref, planes, plane, b_feat, b_mid, b_top,
              z_first, z_second, z_third, z_fourth, z_head)
 
     own = patch * 4 + seg
     first = first_ref[own]
     shift = 3 - offset_ref[own]
-
-    def piece(j):
-        start = shift + 4 * ((j // 4 - first + 256) % 4)
-        value = jnp.concatenate(
-            [planes[pl.ds((j % 4 * 3 + kind) * ROWS + start, 4), :] for kind in range(3)], axis=0)
-        return (value * value).astype(bf16)
-
-    for d in range(16):
-        send_a[d] = piece((mine + d) % 16)
+    starts = [shift + 4 * lax.rem(t - first + 256, 4) for t in turns]
     pl.semaphore_wait(barrier, 34)
-    stage_a = []
-    for n, (h, d) in enumerate(others):
-        copy = pltpu.make_async_remote_copy(
-            src_ref=send_a.at[d], dst_ref=recv_a.at[half * 16 + mine],
-            send_sem=sa_sem.at[n], recv_sem=ra_sem.at[half * 16 + mine],
-            device_id=near((half + h) % 2, (mine + d) % 16), device_id_type=MESH)
-        copy.start()
-        stage_a.append(copy)
-    recv_a[half * 16 + mine] = send_a[0]
-    for n, (h, d) in enumerate(others):
-        j = (half + h) % 2 * 16 + (mine + 16 - d) % 16
+
+    def stage_a(n):
+        h, t, s = others[n]
+        return pltpu.make_async_remote_copy(
+            src_ref=send_a.at[t * 4 + s], dst_ref=recv_a.at[here],
+            send_sem=sa_sem.at[n], recv_sem=ra_sem.at[here],
+            device_id=ids[n], device_id_type=LOGICAL)
+
+    for n, (h, t, s) in enumerate(others):
+        if h:
+            base = segs[s] * (3 * ROWS) + starts[t]
+            value = jnp.concatenate(
+                [planes[pl.ds(base + kind * ROWS, 4), :] for kind in range(3)], axis=0)
+            send_a[t * 4 + s] = (value * value).astype(bf16)
+        stage_a(n).start()
+    recv_a[here] = send_a[0]
+    for n, (h, t, s) in enumerate(others):
+        source = spots[others.index((h, (4 - t) % 4, (4 - s) % 4))]
         pltpu.make_async_remote_copy(
-            src_ref=send_a.at[d], dst_ref=recv_a.at[j],
-            send_sem=sa_sem.at[n], recv_sem=ra_sem.at[j],
-            device_id=near((half + h) % 2, (mine + 16 - d) % 16), device_id_type=MESH).wait_recv()
+            src_ref=send_a.at[t * 4 + s], dst_ref=recv_a.at[source],
+            send_sem=sa_sem.at[n], recv_sem=ra_sem.at[source],
+            device_id=ids[n], device_id_type=LOGICAL).wait_recv()
 
     for j in range(32):
         pieces[16 * j:16 * j + 12, :] = jnp.sqrt(recv_a[j].astype(f32))
@@ -226,7 +235,7 @@
         copy = pltpu.make_async_remote_copy(
             src_ref=send_b.at[d], dst_ref=recv_b.at[d],
             send_sem=sb_sem.at[d], recv_sem=rb_sem.at[d],
-            device_id=along((line + d) % 4), device_id_type=MESH)
+            device_id=device(half, lines[d], turn, seg), device_id_type=LOGICAL)
         copy.start()
         stage_b.append(copy)
 
@@ -240,7 +249,9 @@
         total = total + decode(recv_b[d])
     for r in range(12):
         out_ref[pl.ds(r, 8, stride=12), :] = total[:, r * 128:(r + 1) * 128]
-    for copy in stage_a + stage_b:
+    for n in range(31):
+        stage_a(n).wait_send()
+    for copy in stage_b:
         copy.wait_send()
 
 
@@ -271,18 +282,19 @@
 
     hbm = pl.BlockSpec(memory_space=pltpu.HBM)
     vmem = pl.BlockSpec(memory_space=pltpu.VMEM)
-    smem = pl.BlockSpec(memory_space=pltpu.SMEM)
     V = pltpu.VMEM
     dma = pltpu.SemaphoreType.DMA
     blended = pl.pallas_call(
         kernel,
         out_shape=V((96, 128), f32),
-        in_specs=[hbm] * 11 + [smem] * 3,
+        in_specs=[hbm] * 14,
         out_specs=vmem,
-        scratch_shapes=conv_buffers() + [V((12 * ROWS, 128), f32)] + conv_scratch() + [
+        scratch_shapes=conv_buffers() + [
+            pltpu.SMEM((3,), f32), pltpu.SMEM((128,), jnp.int32), pltpu.SMEM((128,), jnp.int32),
+            V((12 * ROWS, 128), f32)] + conv_scratch() + [
             V((32, 32), f32), V((16, 12, 128), bf16), V((32, 12, 128), bf16), V((512, 128), f32),
             V((4, 8, 1536), bf16), V((4, 8, 1536), bf16),
-            dma((11,)), dma((31,)), dma((32,)), dma((4,)), dma((4,)),
+            dma((14,)), dma((31,)), dma((32,)), dma((4,)), dma((4,)),
         ],
         compiler_params=pltpu.CompilerParams(
             collective_id=0, has_side_effects=True, vmem_limit_bytes=60 << 20),

time: 22.2 us -> 21.5 us (0.968)
  Pallas kernels: 21.3 us -> 20.8 us
    pallas_call x1, Pallas kernels: 21.3 us -> 20.8 us  [per_device(): pl.pallas_call(kernel, out_shape=V((96, 128), f32), in_specs=[hbm] * 14,...]
where the time goes in v4:
time: 21.5 us; the launch traced here: 21.4 us
  Pallas kernels  20.8 us (97%)
  local copies, waits for them, and re-layouts  0.62 us (3%)
    pallas_call x1, Pallas kernels, per_device(): pl.pallas_call(kernel, out_shape=V((96, 128), f32), in_specs=[hbm] * 14,...  20.8 us
    unnamed x1, local copies, waits for them, and re-layouts  0.62 us

profile of v4, /device:TPU:0, one launch (start us, length us, event | category | flops | bytes accessed | tf_op | source)
XLA Modules:
  0.0 21.4 jit_solution(5521082187057158327)
XLA Ops:
  0.0 20.8 %shard_map.136 = f32[96,128]{1,0:T(8,128)S(1)} custom-call(bf16[4,1344,128]{2,1,0:T(8,128)(2,1)} %bitcast.14, bf16[4,1344,128]{2,1,0:T(8,128)(2,1)} %bitcast.15, bf16[9,28,28]{2,1,0:T(8,128)(2,1)} %wf.1, bf16[27,28,28]{2,1,0:T(8,128)(2,1)} %ws.1, bf16[27,28,56]{2,1,0:T(8,128)(2,1)} %wt.1, bf16[27,28,56]{2,1,0:T(8,128)(2,1)} %wo.1, f32[1,28]{1,0:T(1,128)} %bitcast.16, ...), custom_call_target="tpu_custom_call" | custom-call | tf_op jit(solution)/shard_map/pallas_call | solution.py:287
  20.8 0.6 %copy.17 = f32[8,1,3,1,4,128]{5,4,3,2,1,0:T(4,128)} copy(f32[8,1,3,1,4,128]{5,4,3,2,1,0:T(4,128)S(1)} %bitcast.13) | data formatting | bytes 98304

commit v5 on v4

--- a/solution.py
+++ b/solution.py
@@ -81,6 +81,7 @@
             for task, count in beside:
                 for _ in range(count):
                     next(task, None)
+            settle()
             for b in (2 * n, 2 * n + 1):
                 for da in (2, 1, 0):
                     a = b + 1 - da
@@ -89,7 +90,14 @@
                         sums[a] = sums[a] + term if a in sums else term
             for a in (2 * n - 1, 2 * n) + ((11,) if n == 5 else ()):
                 if a >= 0:
-                    emit(a, jnp.maximum(sums.pop(a) + bias, 0.0))
+                    pending.append((emit, a, sums.pop(a), bias))
+
+    pending = []
+
+    def settle():
+        while pending:
+            emit, a, total, bias = pending.pop(0)
+            emit(a, jnp.maximum(total + bias, 0.0))
 
     def run(task):
         for _ in task:
@@ -99,15 +107,13 @@
     run(expand(wfb, z_first, 1, False))
     copies[0].wait()
     run(relayout(fbuf, b_feat, 0))
-    for i in (6, 3, 7, 1):
+    slots()
+    for i in (6, 3, 7, 1, 4, 8, 5, 9, 10):
         copies[i].wait()
     second = expand(wsb, z_second, 1, True)
     deeper = relayout(dbuf, b_mid, 384)
     layer(b_feat, 0, 1, z_first, bf_ref, lambda a, v: put(b_top, 384, a * 128, v), [(second, 2), (deeper, 2)])
     run(second)
-    slots()
-    for i in (4, 8, 5):
-        copies[i].wait()
     third = expand(wtb, z_third, 2, True)
     fourth = expand(wob, z_fourth, 2, True)
     layer(b_top, 384, 1, z_second, bs_ref, lambda a, v: put(b_mid, 0, a * 128, v), [(deeper, 3), (third, 3)])
@@ -115,8 +121,6 @@
     run(third)
     layer(b_mid, 0, 2, z_third, bt_ref, lambda a, v: put(b_top, 0, a * 128, v), [(fourth, 3)])
     run(fourth)
-    copies[9].wait()
-    copies[10].wait()
 
     z_head[...] = jnp.zeros((16, 128), f32)
     head = hw_ref[...].astype(f32)
@@ -135,6 +139,7 @@
         b_feat[0:128, a * 128:(a + 1) * 128] = v.astype(bf16)
 
     layer(b_top, 0, 2, z_fourth, bo_ref, keep)
+    settle()
     logits = jnp.dot(hweight, b_feat[0:128, :], preferred_element_type=f32)
     for a in range(12):
         value = jax.nn.sigmoid(logits[:, a * 128:(a + 1) * 128] + hbias) * (window * bump(a, 12))
@@ -242,6 +247,8 @@
     def decode(x):
         return jnp.sqrt(jnp.sqrt(x.astype(f32)))
 
+    for n in range(31):
+        stage_a(n).wait_send()
     total = decode(send_b[0])
     for copy in stage_b:
         copy.wait_recv()
@@ -249,8 +256,6 @@
         total = total + decode(recv_b[d])
     for r in range(12):
         out_ref[pl.ds(r, 8, stride=12), :] = total[:, r * 128:(r + 1) * 128]
-    for n in range(31):
-        stage_a(n).wait_send()
     for copy in stage_b:
         copy.wait_send()
 

time: 21.5 us -> 21 us (0.977)
  Pallas kernels: 20.8 us -> 20.2 us
    pallas_call x1, Pallas kernels: 20.8 us -> 20.2 us  [per_device(): pl.pallas_call(kernel, out_shape=V((96, 128), f32), in_specs=[hbm] * 14,...]
where the time goes in v5:
time: 21 us; the launch traced here: 20.9 us
  Pallas kernels  20.2 us (96%)
  local copies, waits for them, and re-layouts  0.62 us (3%)
    pallas_call x1, Pallas kernels, per_device(): pl.pallas_call(kernel, out_shape=V((96, 128), f32), in_specs=[hbm] * 14,...  20.2 us
    unnamed x1, local copies, waits for them, and re-layouts  0.62 us

profile of v5, /device:TPU:0, one launch (start us, length us, event | category | flops | bytes accessed | tf_op | source)
XLA Modules:
  0.0 20.9 jit_solution(4282263746647765119)
XLA Ops:
  0.0 20.2 %shard_map.136 = f32[96,128]{1,0:T(8,128)S(1)} custom-call(bf16[4,1344,128]{2,1,0:T(8,128)(2,1)} %bitcast.14, bf16[4,1344,128]{2,1,0:T(8,128)(2,1)} %bitcast.15, bf16[9,28,28]{2,1,0:T(8,128)(2,1)} %wf.1, bf16[27,28,28]{2,1,0:T(8,128)(2,1)} %ws.1, bf16[27,28,56]{2,1,0:T(8,128)(2,1)} %wt.1, bf16[27,28,56]{2,1,0:T(8,128)(2,1)} %wo.1, f32[1,28]{1,0:T(1,128)} %bitcast.16, ...), custom_call_target="tpu_custom_call" | custom-call | tf_op jit(solution)/shard_map/pallas_call | solution.py:292
  20.3 0.6 %copy.17 = f32[8,1,3,1,4,128]{5,4,3,2,1,0:T(4,128)} copy(f32[8,1,3,1,4,128]{5,4,3,2,1,0:T(4,128)S(1)} %bitcast.13) | data formatting | bytes 98304

commit v6 on v5

--- a/solution.py
+++ b/solution.py
@@ -19,6 +19,9 @@
 
 def copies_in(s, hbm, buffers, sems):
     sources = [ref.at[s] if i < 2 else ref for i, ref in enumerate(hbm)]
+    for w in buffers[2:6]:
+        w[:, 16:32, :] = jnp.zeros((w.shape[0], 16, w.shape[2]), bf16)
+    buffers = [w.at[:, 0:28, :] if 1 < i < 6 else w for i, w in enumerate(buffers)]
     copies = [pltpu.make_async_copy(src, dst, sems.at[i])
               for i, (src, dst) in enumerate(zip(sources, buffers))]
     for i in (2, 0, 6, 3, 7, 1, 4, 8, 5, 9, 10):
@@ -62,7 +65,7 @@
                         if abs(zi - zo) > (1 if full else 0):
                             continue
                         tap = 9 * (zi - zo + 1) + t if full else t
-                        dst[da * 128 + zo * 32:da * 128 + zo * 32 + 28, base + zi * 32:base + zi * 32 + 28] = (
+                        dst[da * 128 + zo * 32:da * 128 + zo * 32 + 32, base + zi * 32:base + zi * 32 + 28] = (
                             w[tap, :, part * 28:part * 28 + 28])
                 yield
 
@@ -174,7 +177,6 @@
 
     others = [(h, t, s) for h in (1, 0) for t in (2, 1, 3, 0) for s in (2, 1, 3, 0) if h or t or s]
     ids = [device(halves[h], line, turns[t], segs[s]) for h, t, s in others]
-    spots = [halves[h] * 16 + turns[t] * 4 + segs[s] for h, t, s in others]
     barrier = pltpu.get_barrier_semaphore()
     for peer in ids + [device(half, y, turn, seg) for y in lines[1:]]:
         pl.semaphore_signal(barrier, inc=1, device_id=peer, device_id_type=LOGICAL)
@@ -205,7 +207,7 @@
         h, t, s = others[n]
         return pltpu.make_async_remote_copy(
             src_ref=send_a.at[t * 4 + s], dst_ref=recv_a.at[here],
-            send_sem=sa_sem.at[n], recv_sem=ra_sem.at[here],
+            send_sem=sa_sem, recv_sem=ra_sem,
             device_id=ids[n], device_id_type=LOGICAL)
 
     for n, (h, t, s) in enumerate(others):
@@ -216,12 +218,10 @@
             send_a[t * 4 + s] = (value * value).astype(bf16)
         stage_a(n).start()
     recv_a[here] = send_a[0]
-    for n, (h, t, s) in enumerate(others):
-        source = spots[others.index((h, (4 - t) % 4, (4 - s) % 4))]
-        pltpu.make_async_remote_copy(
-            src_ref=send_a.at[t * 4 + s], dst_ref=recv_a.at[source],
-            send_sem=sa_sem.at[n], recv_sem=ra_sem.at[source],
-            device_id=ids[n], device_id_type=LOGICAL).wait_recv()
+    def all_pieces(ref, sem):
+        return pltpu.make_async_copy(ref.at[pl.ds(0, 31)], ref.at[pl.ds(0, 31)], sem)
+
+    all_pieces(recv_a, ra_sem).wait()
 
     for j in range(32):
         pieces[16 * j:16 * j + 12, :] = jnp.sqrt(recv_a[j].astype(f32))
@@ -247,8 +247,7 @@
     def decode(x):
         return jnp.sqrt(jnp.sqrt(x.astype(f32)))
 
-    for n in range(31):
-        stage_a(n).wait_send()
+    all_pieces(recv_a, sa_sem).wait()
     total = decode(send_b[0])
     for copy in stage_b:
         copy.wait_recv()
@@ -264,7 +263,7 @@
     V = pltpu.VMEM
     return [
         V((1344, 128), bf16), V((1344, 128), bf16),
-        V((9, 28, 28), bf16), V((27, 28, 28), bf16), V((27, 28, 56), bf16), V((27, 28, 56), bf16),
+        V((9, 32, 28), bf16), V((27, 32, 28), bf16), V((27, 32, 56), bf16), V((27, 32, 56), bf16),
         V((1, 28), f32), V((1, 28), f32), V((1, 28), f32), V((1, 28), f32), V((3, 28), bf16),
     ]
 
@@ -299,7 +298,7 @@
             V((12 * ROWS, 128), f32)] + conv_scratch() + [
             V((32, 32), f32), V((16, 12, 128), bf16), V((32, 12, 128), bf16), V((512, 128), f32),
             V((4, 8, 1536), bf16), V((4, 8, 1536), bf16),
-            dma((14,)), dma((31,)), dma((32,)), dma((4,)), dma((4,)),
+            dma((14,)), dma(()), dma(()), dma((4,)), dma((4,)),
         ],
         compiler_params=pltpu.CompilerParams(
             collective_id=0, has_side_effects=True, vmem_limit_bytes=60 << 20),

time: 21 us -> 20.4 us (0.971)
  Pallas kernels: 20.2 us -> 19.7 us
    pallas_call x1, Pallas kernels: 20.2 us -> 19.7 us  [per_device(): pl.pallas_call(kernel, out_shape=V((96, 128), f32), in_specs=[hbm] * 14,...]
where the time goes in v6:
time: 20.4 us; the launch traced here: 20.3 us
  Pallas kernels  19.7 us (97%)
  local copies, waits for them, and re-layouts  0.62 us (3%)
    pallas_call x1, Pallas kernels, per_device(): pl.pallas_call(kernel, out_shape=V((96, 128), f32), in_specs=[hbm] * 14,...  19.7 us
    unnamed x1, local copies, waits for them, and re-layouts  0.62 us

profile of v6, /device:TPU:0, one launch (start us, length us, event | category | flops | bytes accessed | tf_op | source)
XLA Modules:
  0.0 20.3 jit_solution(9299999707935709297)
XLA Ops:
  0.0 19.7 %shard_map.136 = f32[96,128]{1,0:T(8,128)S(1)} custom-call(bf16[4,1344,128]{2,1,0:T(8,128)(2,1)} %bitcast.14, bf16[4,1344,128]{2,1,0:T(8,128)(2,1)} %bitcast.15, bf16[9,28,28]{2,1,0:T(8,128)(2,1)} %wf.1, bf16[27,28,28]{2,1,0:T(8,128)(2,1)} %ws.1, bf16[27,28,56]{2,1,0:T(8,128)(2,1)} %wt.1, bf16[27,28,56]{2,1,0:T(8,128)(2,1)} %wo.1, f32[1,28]{1,0:T(1,128)} %bitcast.16, ...), custom_call_target="tpu_custom_call" | custom-call | tf_op jit(solution)/shard_map/pallas_call | solution.py:291
  19.7 0.6 %copy.17 = f32[8,1,3,1,4,128]{5,4,3,2,1,0:T(4,128)} copy(f32[8,1,3,1,4,128]{5,4,3,2,1,0:T(4,128)S(1)} %bitcast.13) | data formatting | bytes 98304

commit v7 on v6

--- a/solution.py
+++ b/solution.py
@@ -235,28 +235,24 @@
         v = v * v
         send_b[:, :, r * 128:(r + 1) * 128] = (v * v).reshape(4, 8, 128).astype(bf16)
 
-    stage_b = []
     for d in (2, 1, 3):
         copy = pltpu.make_async_remote_copy(
             src_ref=send_b.at[d], dst_ref=recv_b.at[d],
-            send_sem=sb_sem.at[d], recv_sem=rb_sem.at[d],
+            send_sem=sb_sem, recv_sem=rb_sem,
             device_id=device(half, lines[d], turn, seg), device_id_type=LOGICAL)
         copy.start()
-        stage_b.append(copy)
 
     def decode(x):
         return jnp.sqrt(jnp.sqrt(x.astype(f32)))
 
     all_pieces(recv_a, sa_sem).wait()
     total = decode(send_b[0])
-    for copy in stage_b:
-        copy.wait_recv()
+    pltpu.make_async_copy(recv_b.at[pl.ds(1, 3)], recv_b.at[pl.ds(1, 3)], rb_sem).wait()
     for d in range(1, 4):
         total = total + decode(recv_b[d])
     for r in range(12):
         out_ref[pl.ds(r, 8, stride=12), :] = total[:, r * 128:(r + 1) * 128]
-    for copy in stage_b:
-        copy.wait_send()
+    pltpu.make_async_copy(recv_b.at[pl.ds(1, 3)], recv_b.at[pl.ds(1, 3)], sb_sem).wait()
 
 
 def conv_buffers():
@@ -298,7 +294,7 @@
             V((12 * ROWS, 128), f32)] + conv_scratch() + [
             V((32, 32), f32), V((16, 12, 128), bf16), V((32, 12, 128), bf16), V((512, 128), f32),
             V((4, 8, 1536), bf16), V((4, 8, 1536), bf16),
-            dma((14,)), dma(()), dma(()), dma((4,)), dma((4,)),
+            dma((14,)), dma(()), dma(()), dma(()), dma(()),
         ],
         compiler_params=pltpu.CompilerParams(
             collective_id=0, has_side_effects=True, vmem_limit_bytes=60 << 20),

time: 20.4 us -> 20.4 us (level)
  no operation moved by 1% of the time
where the time goes in v7:
time: 20.4 us; the launch traced here: 20.2 us
  Pallas kernels  19.6 us (96%)
  local copies, waits for them, and re-layouts  0.62 us (3%)
    pallas_call x1, Pallas kernels, per_device(): pl.pallas_call(kernel, out_shape=V((96, 128), f32), in_specs=[hbm] * 14,...  19.6 us
    unnamed x1, local copies, waits for them, and re-layouts  0.62 us

profile of v7, /device:TPU:0, one launch (start us, length us, event | category | flops | bytes accessed | tf_op | source)
XLA Modules:
  0.0 20.2 jit_solution(7122622218722723747)
XLA Ops:
  0.0 19.6 %shard_map.136 = f32[96,128]{1,0:T(8,128)S(1)} custom-call(bf16[4,1344,128]{2,1,0:T(8,128)(2,1)} %bitcast.14, bf16[4,1344,128]{2,1,0:T(8,128)(2,1)} %bitcast.15, bf16[9,28,28]{2,1,0:T(8,128)(2,1)} %wf.1, bf16[27,28,28]{2,1,0:T(8,128)(2,1)} %ws.1, bf16[27,28,56]{2,1,0:T(8,128)(2,1)} %wt.1, bf16[27,28,56]{2,1,0:T(8,128)(2,1)} %wo.1, f32[1,28]{1,0:T(1,128)} %bitcast.16, ...), custom_call_target="tpu_custom_call" | custom-call | tf_op jit(solution)/shard_map/pallas_call | solution.py:287
  19.6 0.6 %copy.17 = f32[8,1,3,1,4,128]{5,4,3,2,1,0:T(4,128)} copy(f32[8,1,3,1,4,128]{5,4,3,2,1,0:T(4,128)S(1)} %bitcast.13) | data formatting | bytes 98304

commit v8 on v7

--- a/solution.py
+++ b/solution.py
@@ -227,13 +227,12 @@
         pieces[16 * j:16 * j + 12, :] = jnp.sqrt(recv_a[j].astype(f32))
     hot = hot_ref[...].astype(bf16)
     hot = jnp.concatenate([hot, hot], axis=1)
-    for r in range(12):
-        x = pieces[pl.ds(r, 32, stride=16), :]
-        high = x.astype(bf16)
-        low = (x - high.astype(f32)).astype(bf16)
-        v = jnp.dot(hot, jnp.concatenate([high, low], axis=0), preferred_element_type=f32)
-        v = v * v
-        send_b[:, :, r * 128:(r + 1) * 128] = (v * v).reshape(4, 8, 128).astype(bf16)
+    x = jnp.concatenate([pieces[pl.ds(r, 32, stride=16), :] for r in range(12)], axis=1)
+    high = x.astype(bf16)
+    low = (x - high.astype(f32)).astype(bf16)
+    v = jnp.dot(hot, jnp.concatenate([high, low], axis=0), preferred_element_type=f32)
+    v = v * v
+    send_b[...] = (v * v).reshape(4, 8, 1536).astype(bf16)
 
     for d in (2, 1, 3):
         copy = pltpu.make_async_remote_copy(

time: 20.4 us -> 20.4 us (level)
  no operation moved by 1% of the time
where the time goes in v8:
time: 20.4 us; the launch traced here: 20.2 us
  Pallas kernels  19.6 us (96%)
  local copies, waits for them, and re-layouts  0.62 us (3%)
    pallas_call x1, Pallas kernels, per_device(): pl.pallas_call(kernel, out_shape=V((96, 128), f32), in_specs=[hbm] * 14,...  19.6 us
    unnamed x1, local copies, waits for them, and re-layouts  0.62 us

profile of v8, /device:TPU:0, one launch (start us, length us, event | category | flops | bytes accessed | tf_op | source)
XLA Modules:
  0.0 20.2 jit_solution(11087280675723335603)
XLA Ops:
  0.0 19.6 %shard_map.136 = f32[96,128]{1,0:T(8,128)S(1)} custom-call(bf16[4,1344,128]{2,1,0:T(8,128)(2,1)} %bitcast.14, bf16[4,1344,128]{2,1,0:T(8,128)(2,1)} %bitcast.15, bf16[9,28,28]{2,1,0:T(8,128)(2,1)} %wf.1, bf16[27,28,28]{2,1,0:T(8,128)(2,1)} %ws.1, bf16[27,28,56]{2,1,0:T(8,128)(2,1)} %wt.1, bf16[27,28,56]{2,1,0:T(8,128)(2,1)} %wo.1, f32[1,28]{1,0:T(1,128)} %bitcast.16, ...), custom_call_target="tpu_custom_call" | custom-call | tf_op jit(solution)/shard_map/pallas_call | solution.py:286
  19.6 0.6 %copy.17 = f32[8,1,3,1,4,128]{5,4,3,2,1,0:T(4,128)} copy(f32[8,1,3,1,4,128]{5,4,3,2,1,0:T(4,128)S(1)} %bitcast.13) | data formatting | bytes 98304
